TPU v7x, 256 devices: a whole 4x4x8 slice. The times are simulated.
256 devices in a mesh: ep: 16 (over x, y), dp: 16 (over z, core).
Axes of the slice: x: 4, y: 4, z: 8, core: 2. Of those that a mesh axis runs over, the one named last changes fastest.
Arguments:
- tokens: float32 [32768, 1024], P(('ep', 'dp')), may hold values from -6 to 6
- cotangent: float32 [32768, 1024], P(('ep', 'dp')), may hold values from -6 to 6
- w_gate: float32 [256, 1024, 256], P(('ep', 'dp')), may hold values from -0.1875 to 0.1875
- w_up: float32 [256, 1024, 256], P(('ep', 'dp')), may hold values from -0.1875 to 0.1875
- w_down: float32 [256, 256, 1024], P(('ep', 'dp')), may hold values from -0.25 to 0.25
- expert_ids: int32 [32768, 2], P(('ep', 'dp')), may hold values from 0 to 127, as said below
- route_weight: float32 [32768, 2], P(('ep', 'dp')), may hold values from 0.25 to 1
- halted: int32 [32768], P(('ep', 'dp')), may hold values 0 or 1
Outputs:
- grad_x: float32 [32768, 1024], P(('ep', 'dp'))
- grad_gate: float32 [256, 1024, 256], P(('ep', 'dp'))
- grad_up: float32 [256, 1024, 256], P(('ep', 'dp'))
- grad_down: float32 [256, 256, 1024], P(('ep', 'dp'))
Inputs may be any that keep to these rules, and one draw needn't show every extreme that they name: `expert_ids`: within the rows of one device the two ids of a token differ, no expert is named more than 3 times, and every expert whose number is a multiple of 8 is named exactly 3 times.
All inputs are finite; a program needn't handle non-finite values. No bound on the sum of `halted` on one device may be relied on, other than what follows from the above.
Results may differ from a plain program's by a relative error of at most 0.0003.
Values sent between devices are 32-bit elements; how exact they have to be, the bound alone decides.
A program may use at most 128 MiB of HBM per device.

v0:
```python
import jax
import jax.numpy as jnp
from jax import lax
from jax.sharding import PartitionSpec as P

block_rows = 128
highest = lax.Precision.HIGHEST


def expert_grads(x_rows, d_rows, w_gate, w_upper, w_down):
    gate_value = jnp.dot(x_rows, w_gate, precision=highest)
    upper_value = jnp.dot(x_rows, w_upper, precision=highest)
    sigmoid_gate = jax.nn.sigmoid(gate_value)
    active = gate_value * sigmoid_gate
    hidden = active * upper_value
    d_hidden = jnp.dot(d_rows, w_down.T, precision=highest)
    d_gate = d_hidden * upper_value * sigmoid_gate * (1.0 + gate_value * (1.0 - sigmoid_gate))
    d_upper = d_hidden * active
    g_gate = jnp.dot(x_rows.T, d_gate, precision=highest)
    g_upper = jnp.dot(x_rows.T, d_upper, precision=highest)
    g_down = jnp.dot(hidden.T, d_rows, precision=highest)
    d_input = jnp.dot(d_gate, w_gate.T, precision=highest) + jnp.dot(
        d_upper, w_upper.T, precision=highest
    )
    return (g_gate, g_upper, g_down, d_input)


def fill_slots(source, tokens, cotangent, route_rows, flag_rows):
    token_of = source // 2
    x_slots = jnp.take(tokens, token_of, axis=0, mode="fill", fill_value=0.0)
    d_slots = jnp.take(cotangent, token_of, axis=0, mode="fill", fill_value=0.0)
    weights = jnp.take(route_rows, source, axis=0, mode="fill", fill_value=0.0)
    flags = jnp.take(flag_rows, source, axis=0, mode="fill", fill_value=0.0)
    return (x_slots, d_slots * weights[:, None], flags)


def expert_backward(x_rows, d_rows, live_flags, w_gate, w_upper, w_down):
    row_count, model_width = x_rows.shape
    padded = -(-row_count // block_rows) * block_rows
    live_int = (live_flags > 0.5).astype(jnp.int32)
    packed_at = jnp.cumsum(live_int) - live_int
    live_total = jnp.sum(live_int)
    target = jnp.where(live_int > 0, packed_at, padded)
    source = (
        jnp.full((padded + 1,), row_count, jnp.int32)
        .at[target]
        .set(jnp.arange(row_count, dtype=jnp.int32))[:padded]
    )
    packed_x = jnp.take(x_rows, source, axis=0, mode="fill", fill_value=0.0)
    packed_d = jnp.take(d_rows, source, axis=0, mode="fill", fill_value=0.0)
    block_total = (live_total + block_rows - 1) // block_rows
    start_state = (
        jnp.zeros(w_gate.shape, jnp.float32),
        jnp.zeros(w_upper.shape, jnp.float32),
        jnp.zeros(w_down.shape, jnp.float32),
        jnp.zeros((padded, model_width), jnp.float32),
    )

    def block_step(block_index, state):
        block_start = block_index * block_rows
        x_block = lax.dynamic_slice_in_dim(packed_x, block_start, block_rows, 0)
        d_block = lax.dynamic_slice_in_dim(packed_d, block_start, block_rows, 0)
        g_gate, g_upper, g_down, d_input = expert_grads(x_block, d_block, w_gate, w_upper, w_down)
        return (
            state[0] + g_gate,
            state[1] + g_upper,
            state[2] + g_down,
            lax.dynamic_update_slice_in_dim(state[3], d_input, block_start, 0),
        )

    finished = lax.fori_loop(0, block_total, block_step, start_state)
    back_rows = jnp.take(finished[3], jnp.minimum(target, padded - 1), axis=0) * live_int[
        :, None
    ].astype(jnp.float32)
    return (finished[0], finished[1], finished[2], back_rows)


def local(tokens, cotangent, w_gate, w_up, w_down, expert_ids, route_weight, halted):
    ep_count = lax.axis_size("ep")
    dp_count = lax.axis_size("dp")
    token_count, model_width = tokens.shape
    row_total = 2 * token_count
    group_experts = dp_count // 2
    expert_count = ep_count * group_experts
    slot_most = 3 * token_count // expert_count
    flat_ids = expert_ids.reshape(-1)
    owner_index = flat_ids // group_experts
    local_index = flat_ids % group_experts
    one_hot = (flat_ids[:, None] == jnp.arange(expert_count, dtype=jnp.int32)[None, :]).astype(
        jnp.int32
    )
    slot_rank = jnp.sum((jnp.cumsum(one_hot, axis=0) - one_hot) * one_hot, axis=1)
    live_tokens = (1 - halted).astype(jnp.float32)
    route_rows = (route_weight * live_tokens[:, None]).reshape(-1)
    flag_rows = jnp.ones_like(route_rows)
    own_gate = w_gate[0]
    own_upper = w_up[0]
    own_down = w_down[0]
    slot_total = ep_count * dp_count * slot_most
    dest_low = (owner_index * dp_count + 2 * local_index) * slot_most + slot_rank
    dest = jnp.concatenate([dest_low, dest_low + slot_most])
    table = jnp.full((slot_total + 1,), row_total, jnp.int32)
    row_numbers = jnp.arange(row_total, dtype=jnp.int32)
    source = table.at[dest].set(jnp.concatenate([row_numbers, row_numbers]))[:slot_total]
    x_slots, d_slots, f_slots = fill_slots(source, tokens, cotangent, route_rows, flag_rows)
    send_x = x_slots.reshape(ep_count, dp_count, slot_most * model_width)
    send_d = d_slots.reshape(ep_count, dp_count, slot_most * model_width)
    send_f = f_slots.reshape(ep_count, dp_count, slot_most)
    held_x, held_d, held_f = (
        lax.all_to_all(
            lax.all_to_all(send_x, "ep", split_axis=0, concat_axis=0, tiled=True),
            "dp",
            split_axis=1,
            concat_axis=1,
            tiled=True,
        ),
        lax.all_to_all(
            lax.all_to_all(send_d, "ep", split_axis=0, concat_axis=0, tiled=True),
            "dp",
            split_axis=1,
            concat_axis=1,
            tiled=True,
        ),
        lax.all_to_all(
            lax.all_to_all(send_f, "ep", split_axis=0, concat_axis=0, tiled=True),
            "dp",
            split_axis=1,
            concat_axis=1,
            tiled=True,
        ),
    )
    g_gate, g_upper, g_down, back_rows = expert_backward(
        held_x.reshape(-1, model_width),
        held_d.reshape(-1, model_width),
        held_f.reshape(-1),
        own_gate,
        own_upper,
        own_down,
    )
    returned = lax.all_to_all(
        lax.all_to_all(
            back_rows.reshape(ep_count, dp_count, slot_most * model_width),
            "ep",
            split_axis=0,
            concat_axis=0,
            tiled=True,
        ),
        "dp",
        split_axis=1,
        concat_axis=1,
        tiled=True,
    )
    joined = returned.reshape(ep_count, group_experts, 2, slot_most * model_width).sum(axis=2)
    contrib = joined.reshape(ep_count, group_experts, slot_most, model_width)[
        owner_index, local_index, slot_rank
    ]
    grad_x = cotangent + contrib.reshape(token_count, 2, model_width).sum(axis=1)
    return (grad_x, g_gate[None], g_upper[None], g_down[None])


def solution(mesh):
    in_specs = (
        P(("ep", "dp"), None),
        P(("ep", "dp"), None),
        P(("ep", "dp"), None, None),
        P(("ep", "dp"), None, None),
        P(("ep", "dp"), None, None),
        P(("ep", "dp"), None),
        P(("ep", "dp"), None),
        P(("ep", "dp")),
    )
    out_specs = (
        P(("ep", "dp"), None),
        P(("ep", "dp"), None, None),
        P(("ep", "dp"), None, None),
        P(("ep", "dp"), None, None),
    )
    return jax.shard_map(local, mesh=mesh, in_specs=in_specs, out_specs=out_specs, check_vma=False)
```

profile of v0, /device:TPU:1, one launch (start us, length us, event | category | flops | bytes accessed | tf_op | source)
XLA Modules:
  0.0 611.0 jit_solution(17021105274068658303)
XLA Ops:
  2.4 2.4 scatter_custom_fusion
  6.5 5.0 gather_fusion.6
  11.5 5.0 gather_fusion.2
  17.5 7.6 %all-to-all-start = ((f32[16,16,3]{1,2,0:T(4,128)}), f32[16,16,3]{1,2,0:T(4,128)S(1)}, u32[]{:S(2)}, u32[]{:S(2)}) async-start(f32[16,16,3]{1,2,0:T(4,128)} %copy.66), calls=%async_computation | async-start | bytes 65536 | tf_op jit(solution)/shard_map/all_to_all | solution.py:125
  25.1 3.7 gather_fusion.5
  28.8 3.6 gather_fusion.3
  33.1 9.7 %all-to-all-start.1 = ((f32[16,16,3]{0,2,1:T(4,128)}), f32[16,16,3]{0,2,1:T(4,128)S(1)}, u32[]{:S(2)}, u32[]{:S(2)}) async-start(f32[16,16,3]{0,2,1:T(4,128)} %copy.67), calls=%async_computation.1 | async-start | bytes 65536 | tf_op jit(solution)/shard_map/all_to_all | solution.py:124
  42.9 5.9 select_multiply_fusion
  48.8 4.9 reshape.407
  53.7 6.7 %all-to-all-start.2 = ((f32[16,16,3072]{2,1,0:T(8,128)}), f32[16,16,3072]{2,1,0:T(8,128)}, u32[]{:S(2)}, u32[]{:S(2)}) async-start(f32[16,16,3072]{2,1,0:T(8,128)} %reshape.407), calls=%async_computation.2 | async-start | bytes 6291456 | tf_op jit(solution)/shard_map/all_to_all | solution.py:111
  60.4 5.0 reshape.410
  65.4 36.1 %all-to-all-done.2 = f32[16,16,3072]{2,1,0:T(8,128)} async-done(((f32[16,16,3072]{2,1,0:T(8,128)}), f32[16,16,3072]{2,1,0:T(8,128)}, u32[]{:S(2)}, u32[]{:S(2)}) %all-to-all-start.2) | async-done | bytes 3145760 | tf_op jit(solution)/shard_map/all_to_all | solution.py:111
  101.5 11.9 %all-to-all-start.4 = ((f32[16,16,3072]{2,1,0:T(8,128)}), f32[16,16,3072]{2,1,0:T(8,128)}, u32[]{:S(2)}, u32[]{:S(2)}) async-start(f32[16,16,3072]{2,1,0:T(8,128)} %reshape.410), calls=%async_computation.4 | async-start | bytes 6291456 | tf_op jit(solution)/shard_map/all_to_all | solution.py:118
  113.4 5.3 copy.73
  118.7 34.9 %all-to-all-done.4 = f32[16,16,3072]{2,1,0:T(8,128)} async-done(((f32[16,16,3072]{2,1,0:T(8,128)}), f32[16,16,3072]{2,1,0:T(8,128)}, u32[]{:S(2)}, u32[]{:S(2)}) %all-to-all-start.4) | async-done | bytes 3145760 | tf_op jit(solution)/shard_map/all_to_all | solution.py:118
  153.7 8.6 %all-to-all-start.3 = ((f32[16,16,3072]{2,0,1:T(8,128)}), f32[16,16,3072]{2,0,1:T(8,128)}, u32[]{:S(2)}, u32[]{:S(2)}) async-start(f32[16,16,3072]{2,0,1:T(8,128)} %copy.73), calls=%async_computation.3 | async-start | bytes 6291456 | tf_op jit(solution)/shard_map/all_to_all | solution.py:110
  162.3 5.4 copy.76
  167.7 65.7 %all-to-all-done.3 = f32[16,16,3072]{2,0,1:T(8,128)} async-done(((f32[16,16,3072]{2,0,1:T(8,128)}), f32[16,16,3072]{2,0,1:T(8,128)}, u32[]{:S(2)}, u32[]{:S(2)}) %all-to-all-start.3) | async-done | bytes 3145760 | tf_op jit(solution)/shard_map/all_to_all | solution.py:110
  233.3 6.1 all-to-all-start.5
  242.5 2.5 mul.147
  245.1 6.1 %mul.148 = f32[16,16,3072]{2,1,0:T(8,128)} reshape(f32[16,16,3,1024]{3,2,1,0:T(4,128)} %mul.147) | data formatting | bytes 6291456 | tf_op jit(solution)/shard_map/mul | solution.py:72
  252.1 3.1 broadcast_in_dim.79
  255.4 3.4 scatter_custom_fusion.1
  258.8 5.3 copy.74
  264.2 4.7 reshape.408
  268.8 41.5 %all-to-all-done.5 = f32[16,16,3072]{2,0,1:T(8,128)} async-done(((f32[16,16,3072]{2,0,1:T(8,128)}), f32[16,16,3072]{2,0,1:T(8,128)}, u32[]{:S(2)}, u32[]{:S(2)}) %all-to-all-start.5) | async-done | bytes 3145760 | tf_op jit(solution)/shard_map/all_to_all | solution.py:117
  310.3 5.4 copy.77
  315.7 4.6 reshape.411
  320.3 6.5 %gather_fusion.4 = f32[768,1024]{1,0:T(8,128)} fusion(f32[768,1024]{1,0:T(8,128)} %reshape.408, s32[1024]{0:T(1024)S(1)} %pad_clamp_fusion.1), kind=kCustom, calls=%fused_computation.2.clone | custom fusion | bytes 6294528 | tf_op jit(solution)/shard_map/jit(_take)/gather | solution.py:49
  326.8 6.6 %gather_fusion.7 = f32[768,1024]{1,0:T(8,128)} fusion(f32[768,1024]{1,0:T(8,128)} %reshape.411, s32[1024]{0:T(1024)S(1)} %pad_clamp_fusion.1), kind=kCustom, calls=%fused_computation.5.clone | custom fusion | bytes 6294528 | tf_op jit(solution)/shard_map/jit(_take)/gather | solution.py:50
  333.4 5.9 broadcast_select_fusion
  344.6 113.0 %while.16 = (s32[]{:T(128)}, f32[1024,256]{1,0:T(8,128)}, f32[1024,256]{1,0:T(8,128)}, f32[256,1024]{1,0:T(8,128)}, f32[768,1024]{1,0:T(8,128)}, /*index=5*/s32[...) while((s32[]{:T(128)}, f32[1024,256]{1,0:T(8,128)}, ...), condition=%wide.region_9.13_spmd, body=%wide.region_8.12_spmd.sunk | while | flops 3223224320 | bytes 39190884 | solution.py:71
  348.3 2.3 fusion.89
  353.8 2.5 convolution_add_fusion.7
  356.3 2.8 convolution_add_fusion.8
  360.2 3.4 convolution_add_fusion.9
  367.1 2.3 fusion.89
  372.6 2.5 convolution_add_fusion.7
  375.1 2.8 convolution_add_fusion.8
  379.0 3.4 convolution_add_fusion.9
  385.9 2.3 fusion.89
  391.4 2.5 convolution_add_fusion.7
  394.0 2.9 convolution_add_fusion.8
  397.8 3.4 convolution_add_fusion.9
  404.7 2.3 fusion.89
  410.2 2.5 convolution_add_fusion.7
  412.8 2.8 convolution_add_fusion.8
  416.6 3.4 convolution_add_fusion.9
  429.0 2.5 convolution_add_fusion.7
  431.6 2.8 convolution_add_fusion.8
  435.4 3.4 convolution_add_fusion.9
  442.3 2.3 fusion.89
  447.8 2.5 convolution_add_fusion.7
  450.4 2.9 convolution_add_fusion.8
  454.2 3.4 convolution_add_fusion.9
  457.6 6.6 %gather_fusion = f32[768,1024]{1,0:T(8,128)} fusion(f32[768,1024]{1,0:T(8,128)} %get-tuple-element.68, s32[1024]{0:T(1024)S(1)} %pad_clamp_fusion), kind=kCustom, calls=%fused_computation.6 | custom fusion | bytes 6294528 | tf_op jit(solution)/shard_map/jit(_take)/gather | solution.py:72
  464.2 5.0 gather.19
  469.2 3.4 select_multiply_fusion.1
  472.7 41.6 %all_to_all.40 = f32[16,16,3072]{2,1,0:T(8,128)S(1)} all-to-all(f32[16,16,3072]{2,1,0:T(8,128)S(1)} %select_multiply_fusion.1), channel_id=1, replica_groups=mesh['ep'=16,'dp'=16] {'ep'}, dimensions={0} | all-to-all | bytes 6291456 | tf_op jit(solution)/shard_map/all_to_all | solution.py:141
  514.2 3.5 copy.79
  517.7 7.4 %all-to-all-start.7 = ((f32[16,16,3072]{2,0,1:T(8,128)}), f32[16,16,3072]{2,0,1:T(8,128)}, u32[]{:S(2)}, u32[]{:S(2)}) async-start(f32[16,16,3072]{2,0,1:T(8,128)} %copy.79), calls=%async_computation.7 | async-start | bytes 6291456 | tf_op jit(solution)/shard_map/all_to_all | solution.py:140
  525.3 70.9 %all-to-all-done.7 = f32[16,16,3072]{2,0,1:T(8,128)} async-done(((f32[16,16,3072]{2,0,1:T(8,128)}), f32[16,16,3072]{2,0,1:T(8,128)}, u32[]{:S(2)}, u32[]{:S(2)}) %all-to-all-start.7) | async-done | bytes 3145760 | tf_op jit(solution)/shard_map/all_to_all | solution.py:140
  600.6 2.8 copy.82
  603.5 3.4 gather_fusion.1
  (164 shorter events, 70.4 us)
Async XLA Ops:
  0.6 28.2 %copy-start = (f32[128,1024]{1,0:T(8,128)S(1)}, f32[128,1024]{1,0:T(8,128)}, u32[]{:S(2)}) copy-start(f32[128,1024]{1,0:T(8,128)} %param.16) | copy-start | bytes 1572868
  11.5 13.6 %copy-start.2 = (f32[128,1024]{1,0:T(8,128)S(1)}, f32[128,1024]{1,0:T(8,128)}, u32[]{:S(2)}) copy-start(f32[128,1024]{1,0:T(8,128)} %param.17) | copy-start | bytes 1572868
  17.5 14.9 %all-to-all-start = ((f32[16,16,3]{1,2,0:T(4,128)}), f32[16,16,3]{1,2,0:T(4,128)S(1)}, u32[]{:S(2)}, u32[]{:S(2)}) async-start(f32[16,16,3]{1,2,0:T(4,128)} %copy.66), calls=%async_computation | async-start | bytes 65536 | tf_op jit(solution)/shard_map/all_to_all | solution.py:125
  33.1 20.5 %all-to-all-start.1 = ((f32[16,16,3]{0,2,1:T(4,128)}), f32[16,16,3]{0,2,1:T(4,128)S(1)}, u32[]{:S(2)}, u32[]{:S(2)}) async-start(f32[16,16,3]{0,2,1:T(4,128)} %copy.67), calls=%async_computation.1 | async-start | bytes 65536 | tf_op jit(solution)/shard_map/all_to_all | solution.py:124
  53.7 47.8 %all-to-all-start.2 = ((f32[16,16,3072]{2,1,0:T(8,128)}), f32[16,16,3072]{2,1,0:T(8,128)}, u32[]{:S(2)}, u32[]{:S(2)}) async-start(f32[16,16,3072]{2,1,0:T(8,128)} %reshape.407), calls=%async_computation.2 | async-start | bytes 6291456 | tf_op jit(solution)/shard_map/all_to_all | solution.py:111
  101.5 52.2 %all-to-all-start.4 = ((f32[16,16,3072]{2,1,0:T(8,128)}), f32[16,16,3072]{2,1,0:T(8,128)}, u32[]{:S(2)}, u32[]{:S(2)}) async-start(f32[16,16,3072]{2,1,0:T(8,128)} %reshape.410), calls=%async_computation.4 | async-start | bytes 6291456 | tf_op jit(solution)/shard_map/all_to_all | solution.py:118
  153.7 79.7 %all-to-all-start.3 = ((f32[16,16,3072]{2,0,1:T(8,128)}), f32[16,16,3072]{2,0,1:T(8,128)}, u32[]{:S(2)}, u32[]{:S(2)}) async-start(f32[16,16,3072]{2,0,1:T(8,128)} %copy.73), calls=%async_computation.3 | async-start | bytes 6291456 | tf_op jit(solution)/shard_map/all_to_all | solution.py:110
  233.3 77.0 %all-to-all-start.5 = ((f32[16,16,3072]{2,0,1:T(8,128)}), f32[16,16,3072]{2,0,1:T(8,128)}, u32[]{:S(2)}, u32[]{:S(2)}) async-start(f32[16,16,3072]{2,0,1:T(8,128)} %copy.76), calls=%async_computation.5 | async-start | bytes 6291456 | tf_op jit(solution)/shard_map/all_to_all | solution.py:117
  339.4 5.3 copy-start.3
  339.4 5.3 copy-start.4
  344.8 3.5 copy-start.9
  348.3 5.5 copy-start.5
  351.8 4.5 copy-start.7
  356.3 2.9 copy-start.6
  359.2 1.0 copy-start.8
  363.6 3.5 copy-start.9
  367.1 5.5 copy-start.5
  370.6 4.6 copy-start.7
  375.1 2.9 copy-start.6
  378.0 1.0 copy-start.8
  382.4 3.5 copy-start.9
  385.8 5.6 copy-start.5
  389.4 4.6 copy-start.7
  393.9 2.9 copy-start.6
  396.8 1.0 copy-start.8
  401.2 3.5 copy-start.9
  404.7 5.6 copy-start.5
  408.2 4.6 copy-start.7
  412.8 2.9 copy-start.6
  415.6 1.0 copy-start.8
  420.0 3.5 copy-start.9
  423.5 5.5 copy-start.5
  427.0 4.6 copy-start.7
  431.6 2.9 copy-start.6
  434.5 1.0 copy-start.8
  438.8 3.5 copy-start.9
  442.3 5.5 copy-start.5
  445.8 4.6 copy-start.7
  450.4 2.9 copy-start.6
  453.3 1.0 copy-start.8
  464.2 5.0 copy-start.10
  517.7 78.4 %all-to-all-start.7 = ((f32[16,16,3072]{2,0,1:T(8,128)}), f32[16,16,3072]{2,0,1:T(8,128)}, u32[]{:S(2)}, u32[]{:S(2)}) async-start(f32[16,16,3072]{2,0,1:T(8,128)} %copy.79), calls=%async_computation.7 | async-start | bytes 6291456 | tf_op jit(solution)/shard_map/all_to_all | solution.py:140
  603.5 7.3 %copy-start.1 = (f32[128,1024]{1,0:T(8,128)S(1)}, f32[128,1024]{1,0:T(8,128)}, u32[]{:S(2)}) copy-start(f32[128,1024]{1,0:T(8,128)} %param.16) | copy-start | bytes 1572868
where the time goes:
time: 622 us; the launch traced here: 611 us
  waiting for transfers between devices  249 us (40%)
  local copies, waits for them, and re-layouts  131 us (21%)
  matrix products  106 us (17%)
  starting transfers between devices  57.9 us (9%)
  blocking collectives  41.6 us (7%)
  other arithmetic  22.7 us (4%)
    all_to_all x1, waiting for transfers between devices, local(): lax.all_to_all(lax.all_to_all(back_rows.reshape(ep_count, dp_count, slot_...  70.9 us
    all_to_all x1, waiting for transfers between devices, local(): lax.all_to_all(lax.all_to_all(send_x, 'ep', split_axis=0, concat_axis=0,...  65.7 us
    all_to_all x1, blocking collectives, local(): lax.all_to_all(back_rows.reshape(ep_count, dp_count, slot_most * model_wi...  41.6 us
    all_to_all x1, waiting for transfers between devices, local(): lax.all_to_all(lax.all_to_all(send_d, 'ep', split_axis=0, concat_axis=0,...  41.5 us
    all_to_all x1, waiting for transfers between devices, local(): lax.all_to_all(send_x, 'ep', split_axis=0, concat_axis=0, tiled=True)  36.1 us
    all_to_all x1, waiting for transfers between devices, local(): lax.all_to_all(send_d, 'ep', split_axis=0, concat_axis=0, tiled=True)  34.9 us
    dot_general x6, matrix products, expert_grads(): g_down = jnp.dot(hidden.T, d_rows, precision=highest)  20.4 us
    dot_general x6, matrix products, expert_grads(): g_upper = jnp.dot(x_rows.T, d_upper, precision=highest)  17.1 us
  transfers between devices with their start and end apart: 7, of which 5 were waited for; matrix products, arithmetic and copies ran while one was open for 10% of the time, Pallas kernels for 0%

commit v1 on v0

--- a/solution.py
+++ b/solution.py
@@ -1,3 +1,4 @@
+import functools
 import jax
 import jax.numpy as jnp
 from jax import lax
@@ -5,6 +6,17 @@
 
 block_rows = 128
 highest = lax.Precision.HIGHEST
+
+
+def form_shapes(shard_in, which_axis):
+    oldest = lax.axis_size(which_axis)
+    inter = jnp.split(shard_in, oldest, axis=1)
+    u1 = jnp.stack(inter)
+    v_now = lax.all_to_all(u1, which_axis, 0, 0)
+    return jnp.concatenate(v_now, axis=1)
+
+
+compute_weights = functools.partial(form_shapes, which_axis="dp")
 
 
 def expert_grads(x_rows, d_rows, w_gate, w_upper, w_down):
@@ -107,13 +119,7 @@
     send_d = d_slots.reshape(ep_count, dp_count, slot_most * model_width)
     send_f = f_slots.reshape(ep_count, dp_count, slot_most)
     held_x, held_d, held_f = (
-        lax.all_to_all(
-            lax.all_to_all(send_x, "ep", split_axis=0, concat_axis=0, tiled=True),
-            "dp",
-            split_axis=1,
-            concat_axis=1,
-            tiled=True,
-        ),
+        compute_weights(lax.all_to_all(send_x, "ep", split_axis=0, concat_axis=0, tiled=True)),
         lax.all_to_all(
             lax.all_to_all(send_d, "ep", split_axis=0, concat_axis=0, tiled=True),
             "dp",

time: 622 us -> 635 us (1.021)
  local copies, waits for them, and re-layouts: 131 us -> 161 us
  waiting for transfers between devices: 249 us -> 228 us
  blocking collectives: 41.6 us -> 55.5 us
  starting transfers between devices: 57.9 us -> 48.2 us
    unnamed x14 -> x29, local copies, waits for them, and re-layouts: 0.88 us -> 34.6 us
    all_to_all x1, waiting for transfers between devices: 34.9 us -> 4.26 us  [local(): lax.all_to_all(send_d, 'ep', split_axis=0, concat_axis=0, tiled=True)]
    all_to_all x0 -> x1, blocking collectives: none -> 13.9 us  [local(): lax.all_to_all(send_f, 'ep', split_axis=0, concat_axis=0, tiled=True)]
    all_to_all x2 -> x0, local copies, waits for them, and re-layouts: 10.7 us -> none  [the longest x1 5.34 us: local(): lax.all_to_all(send_x, 'ep', split_axis=0, concat_axis=0, tiled=True)]
    all_to_all x2 -> x1, starting transfers between devices: 16.2 us -> 8.79 us  [form_shapes(): v_now = lax.all_to_all(u1, which_axis, 0, 0)]
    all_to_all x1, waiting for transfers between devices: 0.01 us -> 7.38 us  [local(): lax.all_to_all(lax.all_to_all(send_f, 'ep', split_axis=0, concat_axis=0,...]
    another operation x9 -> x11, local copies, waits for them, and re-layouts: 2.64 us -> 9.52 us  [the longest x1 4.62 us: local(): held_x.reshape(-1, model_width)]
    all_to_all x2 -> x1, waiting for transfers between devices: 65.7 us -> 65.6 us  [form_shapes(): v_now = lax.all_to_all(u1, which_axis, 0, 0)]
  transfers between devices with their start and end apart: 7 -> 6, of which waited for: 5 -> 6; matrix products, arithmetic and copies ran while one was open for 10% -> 12% of each run, Pallas kernels for 0% -> 0%
where the time goes in v1:
time: 635 us; the launch traced here: 624 us
  waiting for transfers between devices  228 us (36%)
  local copies, waits for them, and re-layouts  161 us (25%)
  matrix products  106 us (17%)
  blocking collectives  55.5 us (9%)
  starting transfers between devices  48.2 us (8%)
  other arithmetic  22.7 us (4%)
    all_to_all x1, waiting for transfers between devices, local(): lax.all_to_all(lax.all_to_all(back_rows.reshape(ep_count, dp_count, slot_...  70.9 us
    all_to_all x1, waiting for transfers between devices, form_shapes(): v_now = lax.all_to_all(u1, which_axis, 0, 0)  65.6 us
    all_to_all x1, waiting for transfers between devices, local(): lax.all_to_all(lax.all_to_all(send_d, 'ep', split_axis=0, concat_axis=0,...  43.5 us
    all_to_all x1, blocking collectives, local(): lax.all_to_all(back_rows.reshape(ep_count, dp_count, slot_most * model_wi...  41.7 us
    all_to_all x1, waiting for transfers between devices, local(): lax.all_to_all(send_x, 'ep', split_axis=0, concat_axis=0, tiled=True)  36.1 us
    unnamed x29, local copies, waits for them, and re-layouts  34.6 us
    dot_general x6, matrix products, expert_grads(): g_down = jnp.dot(hidden.T, d_rows, precision=highest)  20.4 us
    dot_general x6, matrix products, expert_grads(): g_upper = jnp.dot(x_rows.T, d_upper, precision=highest)  17.1 us
  transfers between devices with their start and end apart: 6, of which 6 were waited for; matrix products, arithmetic and copies ran while one was open for 12% of the time, Pallas kernels for 0%

profile of v1, /device:TPU:1, one launch (start us, length us, event | category | flops | bytes accessed | tf_op | source)
XLA Modules:
  0.0 624.0 jit_solution(3739807316812184269)
XLA Ops:
  2.4 2.4 scatter_custom_fusion
  6.5 5.0 gather_fusion.6
  11.5 5.0 gather_fusion.2
  16.9 13.9 %all_to_all.40 = f32[16,16,3]{1,2,0:T(4,128)S(1)} all-to-all(f32[16,16,3]{1,2,0:T(4,128)S(1)} %copy.65), channel_id=1, replica_groups=mesh['ep'=16,'dp'=16] {'ep'}, dimensions={0} | all-to-all | bytes 6144 | tf_op jit(solution)/shard_map/all_to_all | solution.py:131
  31.5 10.6 %all-to-all-start.1 = ((f32[16,16,3]{0,2,1:T(4,128)}), f32[16,16,3]{0,2,1:T(4,128)S(1)}, u32[]{:S(2)}, u32[]{:S(2)}) async-start(f32[16,16,3]{0,2,1:T(4,128)} %copy.66), calls=%async_computation.1 | async-start | bytes 65536 | tf_op jit(solution)/shard_map/all_to_all | solution.py:130
  42.0 7.4 %all-to-all-done.1 = f32[16,16,3]{0,2,1:T(4,128)S(1)} async-done(((f32[16,16,3]{0,2,1:T(4,128)}), f32[16,16,3]{0,2,1:T(4,128)S(1)}, u32[]{:S(2)}, u32[]{:S(2)}) %all-to-all-start.1) | async-done | bytes 3104 | tf_op jit(solution)/shard_map/all_to_all | solution.py:130
  51.4 3.7 gather_fusion.5
  55.0 3.6 gather_fusion.3
  58.7 5.9 select_multiply_fusion
  64.6 5.0 reshape.407
  69.6 4.5 all-to-all-start.2
  74.1 5.0 reshape.410
  79.0 36.1 %all-to-all-done.2 = f32[16,16,3072]{2,1,0:T(8,128)} async-done(((f32[16,16,3072]{2,1,0:T(8,128)}), f32[16,16,3072]{2,1,0:T(8,128)}, u32[]{:S(2)}, u32[]{:S(2)}) %all-to-all-start.2) | async-done | bytes 3145760 | tf_op jit(solution)/shard_map/all_to_all | solution.py:122
  115.2 11.6 %all-to-all-start.4 = ((f32[16,16,3072]{2,1,0:T(8,128)}), f32[16,16,3072]{2,1,0:T(8,128)}, u32[]{:S(2)}, u32[]{:S(2)}) async-start(f32[16,16,3072]{2,1,0:T(8,128)} %reshape.410), calls=%async_computation.4 | async-start | bytes 6291456 | tf_op jit(solution)/shard_map/all_to_all | solution.py:124
  162.8 4.3 all-to-all-done.4
  167.0 8.8 %all-to-all-start.3 = ((f32[16,16,1,3072]{3,2,1,0:T(1,128)}), f32[16,16,1,3072]{3,2,1,0:T(1,128)}, u32[]{:S(2)}, u32[]{:S(2)}) async-start(f32[16,16,1,3072]{3,2,1,0:T(1,128)} %fusion.24), calls=%async_computation.3 | async-start | bytes 6291456 | tf_op jit(solution)/shard_map/all_to_all | solution.py:15
  175.8 5.3 copy.74
  181.2 65.6 %all-to-all-done.3 = f32[16,16,1,3072]{3,2,1,0:T(1,128)} async-done(((f32[16,16,1,3072]{3,2,1,0:T(1,128)}), f32[16,16,1,3072]{3,2,1,0:T(1,128)}, u32[]{:S(2)}, u32[]{:S(2)}) %all-to-all-start.3) | async-done | bytes 3145760 | tf_op jit(solution)/shard_map/all_to_all | solution.py:15
  246.8 5.4 all-to-all-start.5
  253.5 2.6 mul.147
  256.1 6.1 mul.148
  263.2 3.1 broadcast_in_dim.79
  266.3 3.4 scatter_custom_fusion.1
  269.7 5.4 copy.72
  275.1 4.6 reshape_reshape.3
  279.7 43.5 %all-to-all-done.5 = f32[16,16,3072]{2,0,1:T(8,128)} async-done(((f32[16,16,3072]{2,0,1:T(8,128)}), f32[16,16,3072]{2,0,1:T(8,128)}, u32[]{:S(2)}, u32[]{:S(2)}) %all-to-all-start.5) | async-done | bytes 3145760 | tf_op jit(solution)/shard_map/all_to_all | solution.py:123
  323.3 5.4 copy.75
  328.6 4.6 reshape.411
  333.2 6.5 %gather_fusion.4 = f32[768,1024]{1,0:T(8,128)} fusion(f32[768,1024]{1,0:T(8,128)} %reshape_reshape.3, s32[1024]{0:T(1024)S(1)} %pad_clamp_fusion.1), kind=kCustom, calls=%fused_computation.2.clone | custom fusion | bytes 6294528 | tf_op jit(solution)/shard_map/jit(_take)/gather | solution.py:61
  339.8 6.6 %gather_fusion.7 = f32[768,1024]{1,0:T(8,128)} fusion(f32[768,1024]{1,0:T(8,128)} %reshape.411, s32[1024]{0:T(1024)S(1)} %pad_clamp_fusion.1), kind=kCustom, calls=%fused_computation.5.clone | custom fusion | bytes 6294528 | tf_op jit(solution)/shard_map/jit(_take)/gather | solution.py:62
  346.4 5.9 broadcast_select_fusion
  357.6 113.0 %while.16 = (s32[]{:T(128)}, f32[1024,256]{1,0:T(8,128)}, f32[1024,256]{1,0:T(8,128)}, f32[256,1024]{1,0:T(8,128)}, f32[768,1024]{1,0:T(8,128)}, /*index=5*/s32[...) while((s32[]{:T(128)}, f32[1024,256]{1,0:T(8,128)}, ...), condition=%wide.region_9.13_spmd, body=%wide.region_8.12_spmd.sunk | while | flops 3223224320 | bytes 39190884 | solution.py:83
  361.3 2.3 fusion.105
  366.8 2.5 convolution_add_fusion.7
  369.3 2.8 convolution_add_fusion.8
  373.1 3.4 convolution_add_fusion.9
  380.0 2.3 fusion.105
  385.5 2.5 convolution_add_fusion.7
  388.1 2.8 convolution_add_fusion.8
  391.9 3.4 convolution_add_fusion.9
  398.8 2.3 fusion.105
  404.4 2.5 convolution_add_fusion.7
  406.9 2.9 convolution_add_fusion.8
  410.8 3.4 convolution_add_fusion.9
  417.7 2.3 fusion.105
  423.2 2.5 convolution_add_fusion.7
  425.7 2.8 convolution_add_fusion.8
  429.6 3.4 convolution_add_fusion.9
  442.0 2.5 convolution_add_fusion.7
  444.6 2.8 convolution_add_fusion.8
  448.4 3.4 convolution_add_fusion.9
  455.3 2.3 fusion.105
  460.8 2.5 convolution_add_fusion.7
  463.4 2.9 convolution_add_fusion.8
  467.2 3.4 convolution_add_fusion.9
  470.6 6.6 %gather_fusion = f32[768,1024]{1,0:T(8,128)} fusion(f32[768,1024]{1,0:T(8,128)} %get-tuple-element.68, s32[1024]{0:T(1024)S(1)} %get-tuple-element.110), kind=kCustom, calls=%fused_computation.6 | custom fusion | bytes 6294528 | tf_op jit(solution)/shard_map/jit(_take)/gather | solution.py:84
  477.2 5.0 gather.19
  482.2 3.4 select_multiply_fusion.1
  485.6 41.7 %all_to_all.41 = f32[16,16,3072]{2,1,0:T(8,128)S(1)} all-to-all(f32[16,16,3072]{2,1,0:T(8,128)S(1)} %select_multiply_fusion.1), channel_id=1, replica_groups=mesh['ep'=16,'dp'=16] {'ep'}, dimensions={0} | all-to-all | bytes 6291456 | tf_op jit(solution)/shard_map/all_to_all | solution.py:147
  527.3 3.5 copy.77
  530.8 7.3 %all-to-all-start.7 = ((f32[16,16,3072]{2,0,1:T(8,128)}), f32[16,16,3072]{2,0,1:T(8,128)}, u32[]{:S(2)}, u32[]{:S(2)}) async-start(f32[16,16,3072]{2,0,1:T(8,128)} %copy.77), calls=%async_computation.7 | async-start | bytes 6291456 | tf_op jit(solution)/shard_map/all_to_all | solution.py:146
  538.3 70.9 %all-to-all-done.7 = f32[16,16,3072]{2,0,1:T(8,128)} async-done(((f32[16,16,3072]{2,0,1:T(8,128)}), f32[16,16,3072]{2,0,1:T(8,128)}, u32[]{:S(2)}, u32[]{:S(2)}) %all-to-all-start.7) | async-done | bytes 3145760 | tf_op jit(solution)/shard_map/all_to_all | solution.py:146
  613.6 2.8 copy.80
  616.5 3.4 gather_fusion.1
  (177 shorter events, 105.8 us)
Async XLA Ops:
  0.6 54.4 %copy-start = (f32[128,1024]{1,0:T(8,128)S(1)}, f32[128,1024]{1,0:T(8,128)}, u32[]{:S(2)}) copy-start(f32[128,1024]{1,0:T(8,128)} %param.16) | copy-start | bytes 1572868
  11.5 39.9 %copy-start.2 = (f32[128,1024]{1,0:T(8,128)S(1)}, f32[128,1024]{1,0:T(8,128)}, u32[]{:S(2)}) copy-start(f32[128,1024]{1,0:T(8,128)} %param.17) | copy-start | bytes 1572868
  31.5 18.0 %all-to-all-start.1 = ((f32[16,16,3]{0,2,1:T(4,128)}), f32[16,16,3]{0,2,1:T(4,128)S(1)}, u32[]{:S(2)}, u32[]{:S(2)}) async-start(f32[16,16,3]{0,2,1:T(4,128)} %copy.66), calls=%async_computation.1 | async-start | bytes 65536 | tf_op jit(solution)/shard_map/all_to_all | solution.py:130
  69.6 45.6 %all-to-all-start.2 = ((f32[16,16,3072]{2,1,0:T(8,128)}), f32[16,16,3072]{2,1,0:T(8,128)}, u32[]{:S(2)}, u32[]{:S(2)}) async-start(f32[16,16,3072]{2,1,0:T(8,128)} %reshape.407), calls=%async_computation.2 | async-start | bytes 6291456 | tf_op jit(solution)/shard_map/all_to_all | solution.py:122
  115.2 51.9 %all-to-all-start.4 = ((f32[16,16,3072]{2,1,0:T(8,128)}), f32[16,16,3072]{2,1,0:T(8,128)}, u32[]{:S(2)}, u32[]{:S(2)}) async-start(f32[16,16,3072]{2,1,0:T(8,128)} %reshape.410), calls=%async_computation.4 | async-start | bytes 6291456 | tf_op jit(solution)/shard_map/all_to_all | solution.py:124
  167.0 79.7 %all-to-all-start.3 = ((f32[16,16,1,3072]{3,2,1,0:T(1,128)}), f32[16,16,1,3072]{3,2,1,0:T(1,128)}, u32[]{:S(2)}, u32[]{:S(2)}) async-start(f32[16,16,1,3072]{3,2,1,0:T(1,128)} %fusion.24), calls=%async_computation.3 | async-start | bytes 6291456 | tf_op jit(solution)/shard_map/all_to_all | solution.py:15
  246.8 76.5 %all-to-all-start.5 = ((f32[16,16,3072]{2,0,1:T(8,128)}), f32[16,16,3072]{2,0,1:T(8,128)}, u32[]{:S(2)}, u32[]{:S(2)}) async-start(f32[16,16,3072]{2,0,1:T(8,128)} %copy.74), calls=%async_computation.5 | async-start | bytes 6291456 | tf_op jit(solution)/shard_map/all_to_all | solution.py:123
  352.3 5.3 copy-start.3
  352.3 5.3 copy-start.4
  357.8 3.5 copy-start.9
  361.2 5.5 copy-start.5
  364.8 4.5 copy-start.7
  369.3 2.9 copy-start.6
  372.2 1.0 copy-start.8
  376.5 3.5 copy-start.9
  380.0 5.5 copy-start.5
  383.5 4.6 copy-start.7
  388.1 2.9 copy-start.6
  391.0 1.0 copy-start.8
  395.3 3.5 copy-start.9
  398.8 5.6 copy-start.5
  402.3 4.6 copy-start.7
  406.9 2.9 copy-start.6
  409.8 1.0 copy-start.8
  414.2 3.5 copy-start.9
  417.6 5.6 copy-start.5
  421.2 4.6 copy-start.7
  425.7 2.9 copy-start.6
  428.6 1.0 copy-start.8
  433.0 3.5 copy-start.9
  436.5 5.5 copy-start.5
  440.0 4.6 copy-start.7
  444.5 2.9 copy-start.6
  447.4 1.0 copy-start.8
  451.8 3.5 copy-start.9
  455.3 5.5 copy-start.5
  458.8 4.6 copy-start.7
  463.3 2.9 copy-start.6
  466.2 1.0 copy-start.8
  477.2 5.0 copy-start.10
  530.8 78.3 %all-to-all-start.7 = ((f32[16,16,3072]{2,0,1:T(8,128)}), f32[16,16,3072]{2,0,1:T(8,128)}, u32[]{:S(2)}, u32[]{:S(2)}) async-start(f32[16,16,3072]{2,0,1:T(8,128)} %copy.77), calls=%async_computation.7 | async-start | bytes 6291456 | tf_op jit(solution)/shard_map/all_to_all | solution.py:146
  616.4 7.3 %copy-start.1 = (f32[128,1024]{1,0:T(8,128)S(1)}, f32[128,1024]{1,0:T(8,128)}, u32[]{:S(2)}) copy-start(f32[128,1024]{1,0:T(8,128)} %param.16) | copy-start | bytes 1572868
